TPU v7x, 128 devices: a whole 4x4x4 slice. The times are simulated.
128 devices in a mesh: azimuth: 16 (over y_hi, z, core), radius: 8 (over x, y_lo).
Axes of the slice: x: 4, y: 4 (y_hi: 2, y_lo: 2; y = y_hi * 2 + y_lo), z: 4, core: 2. Of those that a mesh axis runs over, the one named last changes fastest.
Arguments:
- flow_state: float32 [5, 256, 256, 384], P(None, 'azimuth', 'radius'), may hold values from -6 to 6
- base_state: float32 [5, 256, 256, 384], P(None, 'azimuth', 'radius'), may hold values from -6 to 6
- mean_flow: float32 [2, 256], P(None, 'radius'), may hold values from 0.1 to 0.5
- panel_history: bfloat16 [16, 8, 16, 2016], P('azimuth', 'radius'), may hold values from -6 to 6
- panel_line: int32 [16, 8, 16], P('azimuth', 'radius'), may hold values from 0 to 511
- panel_start: int32 [16, 8, 16], P('azimuth', 'radius'), may hold values from 0 to 352
- panel_count: int32 [16, 8], replicated, may hold values from 2 to 16, as said below
- panel_owner: int32 [16, 8, 16], replicated, may hold values from 0 to 15, as said below
- source_weight: bfloat16 [8, 16384, 4096], P('radius', 'azimuth'), may hold values from -0.046875 to 0.046875
- retarded_time: float32 [128, 64, 64], replicated, may hold values from -0.75 to 0.75
- observer_block: int32 [128], replicated, may hold values from 0 to 127, each once
Outputs:
- next_state: float32 [5, 256, 256, 384], P(None, 'azimuth', 'radius')
- observer_pressure: float32 [128, 2048], P(('azimuth', 'radius'))
Inputs may be any that keep to these rules, and one draw needn't show every extreme that they name: The slots 0 to panel_count[a, b] - 1 of device (a, b) are live. `panel_owner`: entries of slots that are not live are ignored. At most 2 live blocks of one device go to one owner, and in every radius band some owner receives exactly 2 live blocks from every device of the band.
All inputs are finite; a program needn't handle non-finite values.
Results may differ from a plain program's by a relative error of at most 0.00039.
Values may be sent and summed in bfloat16 or wider, within the bound.
No kernel may reach another device: no remote copies, remote signals or barrier semaphores. Data moves between devices by JAX's collectives and lax.ppermute only.
A program may use at most 192 MiB of HBM per device.

v0:
```python
import functools
import math

import jax
import jax.numpy as jnp
from jax import lax
from jax.experimental import pallas as pl
from jax.experimental.pallas import tpu as pltpu
from jax.sharding import PartitionSpec as P

NT = 64
BP = 32
KMAX = 16
CAP = 2
LANES = 128
ROWS = NT * BP // LANES
QUADS = LANES // BP
WIRE_SCALE = 64.0
WIDTH = 1024

SECTION_STEP = 0.3
VISCOSITY = 0.05
BOTH = ("azimuth", "radius")

NVAR = 5
FIRST_RAD = (2, 4)
LATER_RAD = (0, 1, 3)


def swap_quads(tiles):
    lane = lax.broadcasted_iota(jnp.int32, tiles[0].shape, 1)
    low, even = (lane % 128) < 64, (lane % 64) < 32
    a0, a1, a2, a3 = tiles

    def turn(x, shift):
        return pltpu.roll(x, shift, 1)

    b0 = jnp.where(low, a0, turn(a2, 64))
    b2 = jnp.where(low, turn(a0, 64), a2)
    b1 = jnp.where(low, a1, turn(a3, 64))
    b3 = jnp.where(low, turn(a1, 64), a3)
    return (
        jnp.where(even, b0, turn(b1, 32)),
        jnp.where(even, turn(b0, 96), b1),
        jnp.where(even, b2, turn(b3, 32)),
        jnp.where(even, turn(b2, 96), b3),
    )


EDGE = 8
CHUNK = 4


def plane_copies(flow_ref, before_ref, after_ref, ext_ref, sems):
    planes, rows, length = flow_ref.shape[1:]
    sources = [(before_ref, 0, 0, 2)]
    for first in range(0, planes, CHUNK):
        sources.append((flow_ref, first, first + 2, CHUNK))
    sources.append((after_ref, 0, planes + 2, 2))
    stages = []
    for stage, (ref, first, spot, count) in enumerate(sources):
        stages.append([])
        for var in range(NVAR):
            for t in range(length // LANES):
                src = ref.at[var, pl.ds(first, count), :, pl.ds(t * LANES, LANES)]
                dst = ext_ref.at[var, pl.ds(spot, count), t, pl.ds(EDGE, rows)]
                stages[-1].append(pltpu.make_async_copy(src, dst, sems.at[stage, var, t]))
    return stages


def axial_shifts(tiles):
    lane = lax.broadcasted_iota(jnp.int32, tiles[0].shape, 1)
    count = len(tiles)
    shifts = []
    for offset in (1, -1, 2, -2):
        turned = [pltpu.roll(t, (-offset) % LANES, 1) for t in tiles]
        step = 1 if offset > 0 else -1
        outside = lane >= LANES - offset if offset > 0 else lane < -offset
        shifts.append(
            [
                jnp.where(outside, turned[t + step] if 0 <= t + step < count else 0.0, turned[t])
                for t in range(count)
            ]
        )
    return [tuple(s[t] for s in shifts) for t in range(count)]


def plane_update(part, coef, base):
    k8, k1 = SECTION_STEP * 8.0 / 12.0, SECTION_STEP / 12.0
    r1, r2 = SECTION_STEP * VISCOSITY * 16.0 / 12.0, SECTION_STEP * VISCOSITY / 12.0
    c0 = -3.0 * 30.0 / 12.0 * SECTION_STEP * VISCOSITY

    def slope(far, near, p1, m1, p2, m2):
        return near * (p1 - m1) - far * (p2 - m2)

    totals = {}
    extra = {}
    for var in (4, 2, 3, 1, 0):
        centre = part(var, 0, 0)
        axial = axial_shifts(centre)
        cycle = list(zip(*[part(var, d, 0) for d in (1, -1, 2, -2)]))
        band = list(zip(*[part(var, 0, d) for d in (1, -1, 2, -2)]))
        values = base(var)
        totals[var] = []
        for t, x in enumerate(centre):
            total = values[t] + c0 * x
            for i in range(4):
                total += coef(i) * cycle[t][i]
                total += coef(7 + i) * axial[t][i]
            total += r1 * (band[t][0] + band[t][1])
            total -= r2 * (band[t][2] + band[t][3])
            if var == 4:
                extra[1, t] = slope(coef(5), coef(4), *cycle[t])
                extra[2, t] = slope(k1, k8, *band[t])
                extra[3, t] = slope(k1, k8, *axial[t])
            elif var == 2:
                extra[0, t] = slope(k1, k8, *band[t]) + coef(6) * x
            elif var == 3:
                extra[0, t] += slope(k1, k8, *axial[t])
            elif var == 1:
                extra[0, t] += slope(coef(5), coef(4), *cycle[t])
            if var in (1, 2, 3, 0):
                total -= extra[var, t]
            totals[var].append(total)
    for t in range(len(totals[4])):
        totals[4][t] -= extra[0, t]
    return totals


def pack_kernel(flow_ref, *refs, rad, with_az):
    *outs, edge_ref, sems = refs
    rad_first_ref, rad_last_ref = outs[-2:]
    planes, rows = flow_ref.shape[1:3]
    direct, edges = [], []
    for s, var in enumerate(rad):
        for side, start in enumerate((0, rows - EDGE)):
            edges.append(
                pltpu.make_async_copy(
                    flow_ref.at[var, :, pl.ds(start, EDGE)],
                    edge_ref.at[side, s],
                    sems.at[side, s],
                )
            )
    if with_az:
        for side, (ref, start) in enumerate(zip(outs, (0, planes - 2))):
            direct.append(
                pltpu.make_async_copy(
                    flow_ref.at[:, pl.ds(start, 2)], ref, sems.at[side, len(rad)]
                )
            )
    for c in edges + direct:
        c.start()
    for c in edges:
        c.wait()
    for a in range(planes):
        for s in range(len(rad)):
            rad_first_ref[a, 2 * s : 2 * s + 2, :] = edge_ref[0, s, a, 0:2, :]
            rad_last_ref[a, 2 * s : 2 * s + 2, :] = edge_ref[1, s, a, EDGE - 2 : EDGE, :]
    for c in direct:
        c.wait()


def fill_coefficients(coef_ref, mean_ref, planes):
    rows = coef_ref.shape[1]
    dt, nu = SECTION_STEP, VISCOSITY
    eye = lax.broadcasted_iota(jnp.int32, (rows, rows), 0) == lax.broadcasted_iota(
        jnp.int32, (rows, rows), 1
    )

    def column(i):
        spread = jnp.where(eye, mean_ref[i : i + 1, :], 0.0)
        return jnp.broadcast_to(jnp.sum(spread, axis=1, keepdims=True), (rows, LANES))

    cell = lax.broadcasted_iota(jnp.int32, (rows, LANES), 0) + lax.axis_index("radius") * rows
    radius_pos = cell.astype(jnp.float32) + (0.5 * rows * lax.axis_size("radius") + 0.5)
    metric = planes * lax.axis_size("azimuth") / (2.0 * math.pi) / radius_pos
    turn = column(0) * metric
    for at, speed in ((0, turn), (7, column(1))):
        coef_ref[at] = dt * (nu * 16.0 / 12.0 - speed * (8.0 / 12.0))
        coef_ref[at + 1] = dt * (nu * 16.0 / 12.0 + speed * (8.0 / 12.0))
        coef_ref[at + 2] = dt * (speed / 12.0 - nu / 12.0)
        coef_ref[at + 3] = -dt * (speed / 12.0 + nu / 12.0)
    coef_ref[4] = dt * 8.0 / 12.0 * metric
    coef_ref[5] = dt / 12.0 * metric
    coef_ref[6] = dt / radius_pos


def panels_kernel(
    owner_ref,
    count_ref,
    line_ref,
    mean_ref,
    order_ref,
    flow_ref,
    base_ref,
    history_ref,
    out_ref,
    rows_ref,
    coef_ref,
    mask_ref,
    slots_ref,
    store_ref,
    wide_ref,
    block_ref,
    rank_ref,
    own_ref,
    sems,
):
    planes, tiles, band = store_ref.shape[1:4]
    sources = ((flow_ref, 4), (flow_ref, 1), (flow_ref, 2), (flow_ref, 3), (base_ref, 4))
    copies = [
        pltpu.make_async_copy(
            ref.at[var, :, :, pl.ds(t * LANES, LANES)], store_ref.at[s, :, t], sems.at[s, t]
        )
        for s, (ref, var) in enumerate(sources)
        for t in range(tiles)
    ]
    cycle, radius = lax.axis_index("azimuth"), lax.axis_index("radius")
    owners = pltpu.make_async_copy(owner_ref.at[cycle], own_ref, sems.at[len(sources), 0])
    owners.start()
    for c in copies:
        c.start()
    mine = order_ref[cycle * lax.axis_size("radius") + radius]
    block = lax.broadcasted_iota(jnp.int32, mask_ref.shape, 1)
    mask_ref[...] = jnp.where(block == mine, 1.0, 0.0)
    count = count_ref[radius, cycle]
    slots_ref[2 * KMAX] = count
    fill_coefficients(coef_ref, mean_ref, planes)
    wide_ref[ROWS - 1] = jnp.zeros_like(wide_ref[ROWS - 1])
    for r in range(ROWS):
        width = min(LANES, history_ref.shape[1] - r * LANES)
        chunk = history_ref[:, r * LANES : r * LANES + width]
        wide_ref[r, :, 0:width] = chunk.astype(jnp.float32)
    out_ref[...] = jnp.zeros_like(out_ref)

    for q in range(rank_ref.shape[0]):
        rank_ref[q] = 0
    owners.wait()

    def place(k, carry):
        owner = own_ref[radius, k]
        rank = rank_ref[owner]
        rank_ref[owner] = rank + 1
        slots_ref[k] = owner
        slots_ref[KMAX + k] = rank
        for r in range(ROWS):
            block_ref[r : r + 1, :] = wide_ref[r, pl.ds(k, 1), :]
        at = pl.ds(pl.multiple_of(rank * ROWS, ROWS), ROWS)
        out_ref[owner, at, :] = block_ref[...].astype(out_ref.dtype)
        return carry

    lax.fori_loop(0, count, place, 0)
    for c in copies:
        c.wait()

    lane = lax.broadcasted_iota(jnp.int32, (1, LANES), 1)
    k8, k1 = SECTION_STEP * 8.0 / 12.0, SECTION_STEP / 12.0
    r1, r2 = SECTION_STEP * VISCOSITY * 16.0 / 12.0, SECTION_STEP * VISCOSITY / 12.0

    def shifted(x, offset):
        turned = [pltpu.roll(t, (-offset) % LANES, 1) for t in x]
        zero = jnp.zeros_like(x[0])
        if offset < 0:
            return [
                jnp.where(lane < -offset, turned[t - 1] if t else zero, turned[t])
                for t in range(tiles)
            ]
        return [
            jnp.where(lane >= LANES - offset, turned[t + 1] if t + 1 < tiles else zero, turned[t])
            for t in range(tiles)
        ]

    def local(k, carry):
        line = line_ref[0, 0, k]
        la, lr = lax.div(line, band), lax.rem(line, band)

        def row(s, a, r):
            return [store_ref[s, a, t, pl.ds(r, 1), :] for t in range(tiles)]

        def coef(i, inside=None):
            value = coef_ref[i, pl.ds(lr, 1), :]
            return value if inside is None else jnp.where(inside, value, 0.0)

        center = row(0, la, lr)
        total = row(4, la, lr)

        def add(share, x):
            for t in range(tiles):
                total[t] = total[t] + share * x[t]

        add(-3.0 * 30.0 / 12.0 * SECTION_STEP * VISCOSITY, center)
        add(-coef(6), row(2, la, lr))
        turn = {1: -1.0, -1: 1.0, 2: 1.0, -2: -1.0}
        wind = row(3, la, lr)
        for i, offset in enumerate((1, -1, 2, -2)):
            far = abs(offset) == 2
            plane = la + offset
            inside = jnp.logical_and(plane >= 0, plane < planes)
            plane = jnp.clip(plane, 0, planes - 1)
            add(coef(i, inside), row(0, plane, lr))
            add(turn[offset] * coef(5 if far else 4, inside), row(1, plane, lr))
            cell = lr + offset
            inside = jnp.logical_and(cell >= 0, cell < band)
            cell = jnp.clip(cell, 0, band - 1)
            add(jnp.where(inside, -r2 if far else r1, 0.0), row(0, la, cell))
            add(jnp.where(inside, turn[offset] * (k1 if far else k8), 0.0), row(2, la, cell))
            add(coef(7 + i), shifted(center, offset))
            add(turn[offset] * (k1 if far else k8), shifted(wind, offset))
        for t in range(tiles):
            rows_ref[k, t : t + 1, :] = total[t]
        return carry

    lax.fori_loop(0, count, local, 0)


def fresh_kernel(
    slots_ref,
    line_ref,
    start_ref,
    coef_ref,
    rows_ref,
    before_ref,
    after_ref,
    lo_ref,
    hi_ref,
    held_ref,
    out_ref,
    ring_ref,
    sum_ref,
    sems,
):
    tiles, band = ring_ref.shape[1:3]
    planes = lo_ref.shape[0]
    copies = []
    for s, var in enumerate((1, 4)):
        for side, ref in enumerate((before_ref, after_ref)):
            for t in range(tiles):
                src = ref.at[var, :, :, pl.ds(t * LANES, LANES)]
                dst = ring_ref.at[pl.ds(4 * s + 2 * side, 2), t]
                copies.append(pltpu.make_async_copy(src, dst, sems.at[s, side, t]))
    for c in copies:
        c.start()
    out_ref[...] = held_ref[...]
    lane = lax.broadcasted_iota(jnp.int32, (ROWS, LANES), 1)
    row_of = lax.broadcasted_iota(jnp.int32, (ROWS, LANES), 0)
    k8, k1 = SECTION_STEP * 8.0 / 12.0, SECTION_STEP / 12.0
    r1, r2 = SECTION_STEP * VISCOSITY * 16.0 / 12.0, SECTION_STEP * VISCOSITY / 12.0

    def shares(spot, count, near_before, far_before, near_after, far_after):
        first, second = spot == 0, spot == 1
        last, other = spot == count - 1, spot == count - 2
        return (
            jnp.where(first, far_before, 0.0),
            jnp.where(first, near_before, jnp.where(second, far_before, 0.0)),
            jnp.where(last, near_after, jnp.where(other, far_after, 0.0)),
            jnp.where(last, far_after, 0.0),
        )

    def put(k, carry):
        owner, rank = slots_ref[k], slots_ref[KMAX + k]
        line, start = line_ref[0, 0, k], start_ref[0, 0, k]
        la, lr = lax.div(line, band), lax.rem(line, band)
        for t in range(tiles):
            sum_ref[t : t + 1, :] = rows_ref[k, t : t + 1, :]

        @pl.when(jnp.logical_or(la < 2, la >= planes - 2))
        def _():
            c = [coef_ref[i, pl.ds(lr, 1), :] for i in range(6)]
            wind = shares(la, planes, c[4], -c[5], -c[4], c[5])
            own = shares(la, planes, c[1], c[3], c[0], c[2])
            for t in range(tiles):
                total = sum_ref[t : t + 1, :]
                for j in range(4):
                    total += wind[j] * ring_ref[j, t, pl.ds(lr, 1), :]
                    total += own[j] * ring_ref[4 + j, t, pl.ds(lr, 1), :]
                sum_ref[t : t + 1, :] = total

        @pl.when(jnp.logical_or(lr < 2, lr >= band - 2))
        def _():
            wind = shares(lr, band, k8, -k1, -k8, k1)
            own = shares(lr, band, r1, -r2, r1, -r2)
            for t in range(tiles):
                at = slice(t * LANES, (t + 1) * LANES)
                total = sum_ref[t : t + 1, :]
                for j in range(4):
                    ref = lo_ref if j < 2 else hi_ref
                    total += wind[j] * ref[la, j % 2 : j % 2 + 1, at]
                    total += own[j] * ref[la, 2 + j % 2 : 3 + j % 2, at]
                sum_ref[t : t + 1, :] = total

        tile, off = lax.div(start, LANES), lax.rem(start, LANES)
        other = jnp.minimum(tile + 1, tiles - 1)
        shift = lax.rem(2 * LANES - BP - off, LANES)
        x0 = jnp.broadcast_to(sum_ref[pl.ds(tile, 1), :], (ROWS, LANES))
        x1 = jnp.broadcast_to(sum_ref[pl.ds(other, 1), :], (ROWS, LANES))
        window = jnp.where(
            lane < 2 * LANES - BP - off, pltpu.roll(x0, shift, 1), pltpu.roll(x1, shift, 1)
        )
        at = pl.ds(pl.multiple_of(rank * ROWS, ROWS), ROWS)
        block = out_ref[owner, at, :].astype(jnp.float32)
        place = jnp.logical_and(row_of == ROWS - 1, lane >= LANES - BP)
        out_ref[owner, at, :] = jnp.where(place, window, block).astype(out_ref.dtype)
        return carry

    for c in copies:
        c.wait()
    lax.fori_loop(0, slots_ref[2 * KMAX], put, 0)


def fields_kernel(
    flow_ref,
    before_ref,
    after_ref,
    base_ref,
    lo0_ref,
    hi0_ref,
    lo1_ref,
    hi1_ref,
    coef_ref,
    next_ref,
    ext_ref,
    sems,
):
    group = pl.program_id(0)
    planes, rows, length = flow_ref.shape[1:]
    tiles = length // LANES
    stages = plane_copies(flow_ref, before_ref, after_ref, ext_ref, sems)

    def radial_layers(plane, carry):
        for var in range(NVAR):
            if var in FIRST_RAD:
                lo, hi, s = lo0_ref, hi0_ref, FIRST_RAD.index(var)
            else:
                lo, hi, s = lo1_ref, hi1_ref, LATER_RAD.index(var)
            for t in range(tiles):
                at = slice(2 * s, 2 * s + 2), slice(t * LANES, (t + 1) * LANES)
                ext_ref[var, plane + 2, t, EDGE - 2 : EDGE, :] = lo[(plane, *at)]
                ext_ref[var, plane + 2, t, EDGE + rows : EDGE + rows + 2, :] = hi[(plane, *at)]
        return carry

    @pl.when(group == 0)
    def _():
        for stage in stages:
            for c in stage:
                c.start()
        lax.fori_loop(0, planes, radial_layers, 0)
        for c in stages[0] + stages[1]:
            c.wait()

    def one(inner, carry):
        a = group * CHUNK + inner
        for i, stage in enumerate(stages[2:]):

            @pl.when(a == (i + 1) * CHUNK - 2)
            def _():
                for c in stage:
                    c.wait()

        half = 8
        for start in range(0, rows, half):
            at = slice(start, start + half)

            def part(var, offset, row_shift):
                first = EDGE + start + row_shift
                return [
                    ext_ref[var, a + 2 + offset, t, first : first + half, :] for t in range(tiles)
                ]

            held = [coef_ref[i, at, :] for i in range(coef_ref.shape[0])]

            def base(var):
                return [
                    base_ref[var, inner, at, t * LANES : (t + 1) * LANES] for t in range(tiles)
                ]

            totals = plane_update(part, held.__getitem__, base)
            for var in range(NVAR):
                for t in range(tiles):
                    next_ref[var, inner, at, t * LANES : (t + 1) * LANES] = totals[var][t]
        return carry

    lax.fori_loop(0, CHUNK, one, 0)


ANY = pl.BlockSpec(memory_space=pltpu.HBM)
IN_SMEM = pl.BlockSpec(memory_space=pltpu.SMEM)
IN_VMEM = pl.BlockSpec(memory_space=pltpu.VMEM)
MIB = 1 << 20


def limits(mib, **more):
    return pltpu.CompilerParams(vmem_limit_bytes=mib * MIB, **more)


def cost(flops, moved):
    return pl.CostEstimate(flops=flops, bytes_accessed=moved, transcendentals=0)


def in_hbm(array):
    return pltpu.with_memory_space_constraint(array, pltpu.HBM)


def whole(array):
    shape = array.shape
    return pl.BlockSpec(shape, lambda *_: (0,) * len(shape))


def pack_call(flow, rad, with_az):
    nvar, planes, rows, length = flow.shape
    az_shape = jax.ShapeDtypeStruct((nvar, 2, rows, length), jnp.float32)
    rad_shape = jax.ShapeDtypeStruct((planes, 2 * len(rad), length), jnp.float32)
    shapes = (az_shape,) * (2 * with_az) + (rad_shape,) * 2
    return pl.pallas_call(
        functools.partial(pack_kernel, rad=rad, with_az=with_az),
        out_shape=shapes,
        in_specs=[ANY],
        out_specs=(IN_VMEM,) * len(shapes),
        scratch_shapes=[
            pltpu.VMEM((2, len(rad), planes, EDGE, length), jnp.float32),
            pltpu.SemaphoreType.DMA((2, len(rad) + 1)),
        ],
        compiler_params=limits(8),
        cost_estimate=cost(0, 20 * MIB),
    )(in_hbm(flow))


def panels_call(owner, count, line, mean_flow, order, flow, base, history):
    _, planes, rows, length = flow.shape
    owners, tiles = count.shape[1], length // LANES
    return pl.pallas_call(
        panels_kernel,
        name="panels",
        out_shape=(
            jax.ShapeDtypeStruct((owners, CAP * ROWS, LANES), jnp.bfloat16),
            jax.ShapeDtypeStruct((KMAX, 8, LANES), jnp.float32),
            jax.ShapeDtypeStruct((11, rows, LANES), jnp.float32),
            jax.ShapeDtypeStruct((1, order.shape[0]), jnp.float32),
            jax.ShapeDtypeStruct((LANES,), jnp.int32),
        ),
        in_specs=[ANY, IN_SMEM, IN_SMEM, IN_VMEM, IN_SMEM, ANY, ANY, IN_VMEM],
        out_specs=(IN_VMEM,) * 4 + (IN_SMEM,),
        scratch_shapes=[
            pltpu.VMEM((5, planes, tiles, rows, LANES), jnp.float32),
            pltpu.VMEM((ROWS, KMAX, LANES), jnp.float32),
            pltpu.VMEM((ROWS, LANES), jnp.float32),
            pltpu.SMEM((owners,), jnp.int32),
            pltpu.SMEM(owner.shape[1:], jnp.int32),
            pltpu.SemaphoreType.DMA((6, tiles)),
        ],
        compiler_params=limits(8),
        cost_estimate=cost(0, 5 * 4 * planes * rows * length),
    )(in_hbm(owner), count, line, mean_flow, order, in_hbm(flow), in_hbm(base), history)


def fresh_call(slots, line, start, coef, rows, az, rad, held):
    length = az[0].shape[-1]
    band = az[0].shape[2]
    return pl.pallas_call(
        fresh_kernel,
        name="fresh",
        out_shape=jax.ShapeDtypeStruct(held.shape, held.dtype),
        in_specs=[IN_SMEM] * 3 + [IN_VMEM] * 2 + [pl.BlockSpec(memory_space=pl.ANY)] * 2 + [IN_VMEM] * 3,
        out_specs=IN_VMEM,
        scratch_shapes=[
            pltpu.VMEM((8, length // LANES, band, LANES), jnp.float32),
            pltpu.VMEM((8, LANES), jnp.float32),
            pltpu.SemaphoreType.DMA((2, 2, length // LANES)),
        ],
        compiler_params=limits(8),
        cost_estimate=cost(0, 4 * 4 * band * length * 4),
    )(slots, line, start, coef, rows, *az, *rad, held)


def fields_call(flow, az, base, rad0, rad1, coef):
    nvar, planes, rows, length = flow.shape
    cells = planes * rows * length
    every = (nvar, CHUNK, rows, length)
    args = (in_hbm(flow), *az, in_hbm(base), *rad0, *rad1, coef)
    return pl.pallas_call(
        fields_kernel,
        name="fields",
        out_shape=jax.ShapeDtypeStruct(flow.shape, jnp.float32),
        grid=(planes // CHUNK,),
        in_specs=[
            *[ANY] + [pl.BlockSpec(memory_space=pl.ANY)] * 2,
            pl.BlockSpec(every, lambda a: (0, a, 0, 0)),
            *[whole(x) for x in (*rad0, *rad1, coef)],
        ],
        out_specs=pl.BlockSpec(every, lambda a: (0, a, 0, 0)),
        scratch_shapes=[
            pltpu.VMEM(
                (nvar, planes + 4, length // LANES, rows + 2 * EDGE, LANES), jnp.float32
            ),
            pltpu.SemaphoreType.DMA((planes // CHUNK + 2, nvar, length // LANES)),
        ],
        compiler_params=limits(18, dimension_semantics=("arbitrary",)),
        cost_estimate=cost(250 * cells, 15 * 4 * cells),
    )(*args)


def weights_kernel(
    stations_ref,
    order_ref,
    weight_ref,
    out_ref,
    lhs_ref,
    held_ref,
    order_held_ref,
    spot_ref,
    sems,
):
    chunks, _, width = held_ref.shape
    copies = [
        pltpu.make_async_copy(
            weight_ref.at[:, pl.ds(i * width, width)], held_ref.at[i], sems.at[i]
        )
        for i in range(chunks)
    ]
    orders = pltpu.make_async_copy(order_ref, order_held_ref, sems.at[chunks])
    orders.start()
    for c in copies:
        c.start()
    for group in range(stations_ref.shape[0] * CAP // QUADS):
        tiles = []
        for m in range(QUADS):
            source, rank = divmod(group * QUADS + m, CAP)
            tile = stations_ref[source, rank * ROWS : (rank + 1) * ROWS, :]
            tiles.append(tile.astype(jnp.float32))
        for i, tile in enumerate(swap_quads(tiles)):
            lhs_ref[i * ROWS : (i + 1) * ROWS, group * LANES : (group + 1) * LANES] = tile.astype(
                lhs_ref.dtype
            )

    def place(j, carry):
        spot_ref[order_held_ref[j]] = j
        return carry

    orders.wait()
    lax.fori_loop(0, out_ref.shape[0], place, 0, unroll=8)
    groups = width // LANES
    for n, c in enumerate(copies):
        c.wait()
        part = jnp.dot(lhs_ref[...], held_ref[n], preferred_element_type=jnp.float32)
        for group in range(groups):
            lanes = slice(group * LANES, (group + 1) * LANES)
            tiles = [part[i * ROWS : (i + 1) * ROWS, lanes] for i in range(QUADS)]
            for m, tile in enumerate(swap_quads(tiles)):
                out_ref[spot_ref[(n * groups + group) * QUADS + m]] = tile


def weights_call(order, stations, weight):
    count = order.shape[0]
    depth, observers = weight.shape
    chunks = observers // WIDTH
    return pl.pallas_call(
        weights_kernel,
        name="observers",
        out_shape=jax.ShapeDtypeStruct((count, ROWS, LANES), jnp.float32),
        in_specs=[IN_VMEM, ANY, ANY],
        out_specs=IN_VMEM,
        scratch_shapes=[
            pltpu.VMEM((NT, depth), jnp.bfloat16),
            pltpu.VMEM((chunks, depth, WIDTH), jnp.bfloat16),
            pltpu.SMEM((count,), jnp.int32),
            pltpu.SMEM((count,), jnp.int32),
            pltpu.SemaphoreType.DMA((chunks + 1,)),
        ],
        compiler_params=limits(14),
        cost_estimate=cost(2 * NT * depth * observers, 2 * depth * observers),
    )(stations, in_hbm(order), in_hbm(weight))


def retard_kernel(total_ref, matrix_ref, out_ref, times_ref, late_ref):
    total = total_ref[...]
    for i in range(QUADS):
        turned = total if i == 0 else pltpu.roll(total, LANES - i * BP, 1)
        times_ref[pl.ds(i, ROWS, stride=QUADS), :] = turned
    late_ref[...] = jnp.dot(
        matrix_ref[...],
        times_ref[...],
        precision=lax.Precision.HIGHEST,
        preferred_element_type=jnp.float32,
    )
    lane = lax.broadcasted_iota(jnp.int32, (ROWS, LANES), 1)
    out = late_ref[pl.ds(0, ROWS, stride=QUADS), :]
    for i in range(1, QUADS):
        tile = pltpu.roll(late_ref[pl.ds(i, ROWS, stride=QUADS), :], i * BP, 1)
        out = jnp.where(lane >= i * BP, tile, out)
    out_ref[...] = out


def retard_call(total, matrix):
    return pl.pallas_call(
        retard_kernel,
        name="retard",
        out_shape=jax.ShapeDtypeStruct((ROWS, LANES), jnp.float32),
        in_specs=[pl.BlockSpec(memory_space=pltpu.VMEM)] * 2,
        out_specs=pl.BlockSpec(memory_space=pltpu.VMEM),
        scratch_shapes=[pltpu.VMEM((NT, LANES), jnp.float32)] * 2,
        compiler_params=limits(4),
        cost_estimate=cost(2 * NT * NT * LANES, 4 * NT * NT),
    )(total, matrix)


def exchange(first, last, axis, wrap):
    count = lax.axis_size(axis)
    up = [(i, (i + 1) % count) for i in range(count if wrap else count - 1)]
    down = [(j, i) for i, j in up]
    return lax.ppermute(last, axis, up), lax.ppermute(first, axis, down)


def per_device(
    flow_state,
    base_state,
    mean_flow,
    panel_history,
    panel_line,
    panel_start,
    panel_count,
    panel_owner,
    source_weight,
    retarded_time,
    observer_block,
):
    az_first, az_last, *ends = pack_call(flow_state, FIRST_RAD, True)
    az = exchange(az_first, az_last, "azimuth", True)
    rad0 = exchange(*ends, "radius", False)
    history, local, coef, mask, slots = panels_call(
        panel_owner,
        panel_count.T,
        panel_line,
        mean_flow,
        observer_block,
        flow_state,
        base_state,
        panel_history[0, 0],
    )
    outgoing = fresh_call(slots, panel_line, panel_start, coef, local, az, rad0, history)
    stations = lax.all_to_all(outgoing, "azimuth", split_axis=0, concat_axis=0, tiled=True)
    later, _ = lax.optimization_barrier((flow_state, outgoing))
    packed = pack_call(later, LATER_RAD, False)
    rad1 = exchange(*packed, "radius", False)
    times, _ = lax.optimization_barrier((retarded_time, outgoing))
    matrix = jnp.sum(times * mask[0][:, None, None], axis=0)
    sends = weights_call(observer_block, stations, source_weight[0])
    sends = (WIRE_SCALE * sends).astype(jnp.float16)
    parts = lax.all_to_all(sends, BOTH, split_axis=0, concat_axis=0, tiled=True)
    next_state = fields_call(flow_state, az, base_state, rad0, rad1, coef)

    total = (1.0 / WIRE_SCALE) * jnp.sum(parts.astype(jnp.float32), axis=0)
    pressure = retard_call(total, matrix)
    return next_state, pressure.reshape(1, ROWS * LANES)


def solution(mesh):
    placed = (
        P(None, "azimuth", "radius", None),
        P(None, "azimuth", "radius", None),
        P(None, "radius"),
        P("azimuth", "radius", None, None),
        P("azimuth", "radius", None),
        P("azimuth", "radius", None),
        P(),
        P(),
        P("radius", "azimuth", None),
        P(),
        P(),
    )

    return jax.shard_map(
        per_device,
        mesh=mesh,
        in_specs=placed,
        out_specs=(P(None, "azimuth", "radius", None), P(BOTH, None)),
        check_vma=False,
    )
```

profile of v0, /device:TPU:3, one launch (start us, length us, event | category | flops | bytes accessed | tf_op | source)
XLA Modules:
  0.0 73.8 jit_solution(17138489501882182972)
XLA Ops:
  0.6 0.0 copy-start.3
  0.7 1.6 %shard_map.122 = (f32[5,2,32,384]{3,2,1,0:T(8,128)S(1)}, f32[5,2,32,384]{3,2,1,0:T(8,128)S(1)}, f32[16,4,384]{2,1,0:T(4,128)S(1)}, f32[16,4,384]{2,1,0:T(4,128)S(1)}) custom-call(f32[5,16,32,384]{3,2,1,0:T(8,128)} %flow_ref.6), custom_call_target="tpu_custom_call" | custom-call | bytes 20971520 | tf_op jit(solution)/shard_map/pallas_call | solution.py:513
  2.3 2.3 %collective-permute-start = (f32[5,2,32,384]{3,2,1,0:T(8,128)S(1)}, f32[5,2,32,384]{3,2,1,0:T(8,128)S(1)}, u32[]{:S(2)}, u32[]{:S(2)}) collective-permute-start(f32[5,2,32,384]{3,2,1,0:T(8,128)S(1)} %get-tuple-element.15), channel_id=1, source_target_pairs={{0,8},{8,16},{16,24},{24,32},{32,40},{40,48},{48,56},{56,64},{64,7... | collective-permute-start | bytes 1474568 | tf_op jit(solution)/shard_map/ppermute | solution.py:709
  4.6 3.2 %collective-permute-start.2 = (f32[16,4,384]{2,1,0:T(4,128)S(1)}, f32[16,4,384]{2,1,0:T(4,128)S(1)}, u32[]{:S(2)}, u32[]{:S(2)}) collective-permute-start(f32[16,4,384]{2,1,0:T(4,128)S(1)} %get-tuple-element.17), channel_id=1, source_target_pairs={{0,1},{1,2},{2,3},{3,4},{4,5},{5,6},{6,7},{8,9},{9,10},{10,11},{11... | collective-permute-start | bytes 294920 | tf_op jit(solution)/shard_map/ppermute | solution.py:709
  7.8 3.0 %collective-permute-start.3 = (f32[16,4,384]{2,1,0:T(4,128)S(1)}, f32[16,4,384]{2,1,0:T(4,128)S(1)}, u32[]{:S(2)}, u32[]{:S(2)}) collective-permute-start(f32[16,4,384]{2,1,0:T(4,128)S(1)} %get-tuple-element.18), channel_id=1, source_target_pairs={{1,0},{2,1},{3,2},{4,3},{5,4},{6,5},{7,6},{9,8},{10,9},{11,10},{12... | collective-permute-start | bytes 294920 | tf_op jit(solution)/shard_map/ppermute | solution.py:709
  10.8 0.0 copy-start.5
  10.8 4.7 %panels.1 = (bf16[16,32,128]{2,1,0:T(8,128)(2,1)S(1)}, f32[16,8,128]{2,1,0:T(8,128)S(1)}, f32[11,32,128]{2,1,0:T(8,128)S(1)}, f32[1,128]{1,0:T(1,128)S(1)}, s32[128]{0:T(128)S(1)}) custom-call(s32[16,8,16]{2,1,0:T(8,128)} %owner_ref.1, s32[8,16]{1,0:T(8,128)S(1)} %bitcast.6, s32[1,1,16]{2,1,0:T(1,128)S(1)} %copy-done.2, f32[2,32]{1,0:T(2,128)S(1)} %copy-done.4, ...), custom_call_target="tpu_custom_call" | custom-call | bytes 3932160 | tf_op jit(solution)/shard_map/panels/pallas_call | solution.py:530
  15.6 0.0 collective-permute-done.3.hi_ref.hi0_ref
  15.6 0.0 collective-permute-done.before_ref
  15.6 1.8 %fresh.1 = bf16[16,32,128]{2,1,0:T(8,128)(2,1)S(1)} custom-call(s32[128]{0:T(128)S(1)} %get-tuple-element.19.slots_ref, s32[1,1,16]{2,1,0:T(1,128)S(1)} %copy-done.2, s32[1,1,16]{2,1,0:T(1,128)S(1)} %copy-done.5, f32[11,32,128]{2,1,0:T(8,128)S(1)} %get-tuple-element.20.coef_ref, f32[16,8,128]{2,1,0:T(8,128)S(1)} %get-tuple-element.21.rows_ref, ...), custom_call_target="tpu_custom_call" | custom-call | bytes 786432 | tf_op jit(solution)/shard_map/fresh/pallas_call | solution.py:558
  17.4 17.0 %all_to_all.10.stations_ref = bf16[16,32,128]{2,1,0:T(8,128)(2,1)S(1)} all-to-all(bf16[16,32,128]{2,1,0:T(8,128)(2,1)S(1)} %fresh.1), channel_id=1, replica_groups=mesh['azimuth'=16,'radius'=8] {'azimuth'}, dimensions={0} | all-to-all | bytes 262144 | tf_op jit(solution)/shard_map/all_to_all | solution.py:739
  34.4 4.2 %observers.1 = f32[128,16,128]{2,1,0:T(8,128)S(1)} custom-call(bf16[16,32,128]{2,1,0:T(8,128)(2,1)S(1)} %all_to_all.10.stations_ref, s32[128]{0:T(128)} %order_ref.3, bf16[1024,4096]{1,0:T(8,128)(2,1)} %bitcast.8), custom_call_target="tpu_custom_call" | custom-call | flops 536870912 | bytes 8388608 | tf_op jit(solution)/shard_map/observers/pallas_call | solution.py:655
  38.7 0.0 copy-start.6
  38.7 0.9 %multiply_convert_fusion = f16[128,16,128]{2,1,0:T(8,128)(2,1)} fusion(f32[128,16,128]{2,1,0:T(8,128)S(1)} %observers.1), kind=kLoop, calls=%fused_computation.2 | loop fusion | flops 524288 | bytes 1572864 | tf_op jit(solution)/shard_map/convert_element_type | solution.py:746
  39.6 4.9 %all-to-all-start.1 = ((f16[128,16,128]{2,1,0:T(8,128)(2,1)}), f16[128,16,128]{2,1,0:T(8,128)(2,1)}, u32[]{:S(2)}, u32[]{:S(2)}) async-start(f16[128,16,128]{2,1,0:T(8,128)(2,1)} %multiply_convert_fusion), calls=%async_computation.1 | async-start | bytes 1048576 | tf_op jit(solution)/shard_map/all_to_all | solution.py:747
  44.5 1.5 %shard_map.123 = (f32[16,6,384]{2,1,0:T(8,128)S(1)}, f32[16,6,384]{2,1,0:T(8,128)S(1)}) custom-call(f32[5,16,32,384]{3,2,1,0:T(8,128)} %flow_ref.6), custom_call_target="tpu_custom_call" | custom-call | bytes 20971520 | tf_op jit(solution)/shard_map/pallas_call | solution.py:513
  46.1 3.1 %collective-permute-start.4 = (f32[16,6,384]{2,1,0:T(8,128)S(1)}, f32[16,6,384]{2,1,0:T(8,128)S(1)}, u32[]{:S(2)}, u32[]{:S(2)}) collective-permute-start(f32[16,6,384]{2,1,0:T(8,128)S(1)} %get-tuple-element.24), channel_id=1, source_target_pairs={{0,1},{1,2},{2,3},{3,4},{4,5},{5,6},{6,7},{8,9},{9,10},{10,11},{11... | collective-permute-start | bytes 442376 | tf_op jit(solution)/shard_map/ppermute | solution.py:709
  49.2 3.1 %collective-permute-start.5 = (f32[16,6,384]{2,1,0:T(8,128)S(1)}, f32[16,6,384]{2,1,0:T(8,128)S(1)}, u32[]{:S(2)}, u32[]{:S(2)}) collective-permute-start(f32[16,6,384]{2,1,0:T(8,128)S(1)} %get-tuple-element.25), channel_id=1, source_target_pairs={{1,0},{2,1},{3,2},{4,3},{5,4},{6,5},{7,6},{9,8},{10,9},{11,10},{12... | collective-permute-start | bytes 442376 | tf_op jit(solution)/shard_map/ppermute | solution.py:709
  52.3 0.6 multiply_reduce_fusion.matrix_ref
  52.9 2.5 %collective-permute-done.4.lo1_ref = f32[16,6,384]{2,1,0:T(8,128)S(1)} collective-permute-done((f32[16,6,384]{2,1,0:T(8,128)S(1)}, f32[16,6,384]{2,1,0:T(8,128)S(1)}, u32[]{:S(2)}, u32[]{:S(2)}) %collective-permute-start.4) | collective-permute-done | bytes 147488 | tf_op jit(solution)/shard_map/ppermute | solution.py:709
  55.4 5.0 %collective-permute-done.5.hi1_ref = f32[16,6,384]{2,1,0:T(8,128)S(1)} collective-permute-done((f32[16,6,384]{2,1,0:T(8,128)S(1)}, f32[16,6,384]{2,1,0:T(8,128)S(1)}, u32[]{:S(2)}, u32[]{:S(2)}) %collective-permute-start.5) | collective-permute-done | bytes 147488 | tf_op jit(solution)/shard_map/ppermute | solution.py:709
  60.4 11.3 %fields.1 = f32[5,16,32,384]{3,2,1,0:T(8,128)} custom-call(f32[5,16,32,384]{3,2,1,0:T(8,128)} %flow_ref.6, f32[5,2,32,384]{3,2,1,0:T(8,128)S(1)} %collective-permute-done.before_ref, f32[5,2,32,384]{3,2,1,0:T(8,128)S(1)} %collective-permute-done.1.after_ref, f32[5,16,32,384]{3,2,1,0:T(8,128)} %base_ref.3, ...), custom_call_target="tpu_custom_call" | custom-call | flops 49152000 | bytes 11796480 | tf_op jit(solution)/shard_map/fields/pallas_call | solution.py:579
  71.7 1.2 %convert_reduce_fusion = f32[16,128]{1,0:T(8,128)S(1)} fusion(f16[128,16,128]{2,1,0:T(8,128)(2,1)} %all-to-all-done.1), kind=kLoop, calls=%fused_computation.1 | loop fusion | flops 522240 | bytes 532480 | tf_op jit(solution)/shard_map/reduce_sum | solution.py:750
  72.9 0.9 %retard.1 = f32[16,128]{1,0:T(8,128)} custom-call(f32[16,128]{1,0:T(8,128)S(1)} %broadcast_multiply_fusion.total_ref, f32[64,64]{1,0:T(8,128)S(1)} %multiply_reduce_fusion.matrix_ref), custom_call_target="tpu_custom_call" | custom-call | flops 1048576 | bytes 16384 | tf_op jit(solution)/shard_map/retard/pallas_call | solution.py:693
  (16 shorter events, 0.0 us)
Async XLA Ops:
  0.6 10.1 %copy-start.3 = (s32[128]{0:T(128)S(1)}, s32[128]{0:T(128)}, u32[]{:S(2)}) copy-start(s32[128]{0:T(128)} %order_ref.3) | copy-start | bytes 1540
  0.6 10.1 %copy-start.2 = (s32[1,1,16]{2,1,0:T(1,128)S(1)}, s32[1,1,16]{2,1,0:T(1,128)}, u32[]{:S(2)}) copy-start(s32[1,1,16]{2,1,0:T(1,128)} %line_ref.3) | copy-start | bytes 196
  0.7 10.1 %copy-start.1 = (s32[16,8]{0,1:T(8,128)S(1)}, s32[16,8]{0,1:T(8,128)}, u32[]{:S(2)}) copy-start(s32[16,8]{0,1:T(8,128)} %param.17) | copy-start | bytes 1540
  0.7 10.1 %copy-start = (bf16[1,1,16,2016]{3,2,1,0:T(8,128)(2,1)S(1)}, bf16[1,1,16,2016]{3,2,1,0:T(8,128)(2,1)}, u32[]{:S(2)}) copy-start(bf16[1,1,16,2016]{3,2,1,0:T(8,128)(2,1)} %param.14) | copy-start | bytes 193540
  0.7 10.1 %copy-start.4 = (f32[2,32]{1,0:T(2,128)S(1)}, f32[2,32]{1,0:T(2,128)}, u32[]{:S(2)}) copy-start(f32[2,32]{1,0:T(2,128)} %mean_ref.1) | copy-start | bytes 772
  2.3 13.3 %collective-permute-start = (f32[5,2,32,384]{3,2,1,0:T(8,128)S(1)}, f32[5,2,32,384]{3,2,1,0:T(8,128)S(1)}, u32[]{:S(2)}, u32[]{:S(2)}) collective-permute-start(f32[5,2,32,384]{3,2,1,0:T(8,128)S(1)} %get-tuple-element.15), channel_id=1, source_target_pairs={{0,8},{8,16},{16,24},{24,32},{32,40},{40,48},{48,56},{56,64},{64,7... | collective-permute-start | bytes 1474568 | tf_op jit(solution)/shard_map/ppermute | solution.py:709
  4.6 11.0 %collective-permute-start.1 = (f32[5,2,32,384]{3,2,1,0:T(8,128)S(1)}, f32[5,2,32,384]{3,2,1,0:T(8,128)S(1)}, u32[]{:S(2)}, u32[]{:S(2)}) collective-permute-start(f32[5,2,32,384]{3,2,1,0:T(8,128)S(1)} %get-tuple-element.16), channel_id=1, source_target_pairs={{8,0},{16,8},{24,16},{32,24},{40,32},{48,40},{56,48},{64,56},{72,6... | collective-permute-start | bytes 1474568 | tf_op jit(solution)/shard_map/ppermute | solution.py:709
  4.6 11.0 %collective-permute-start.2 = (f32[16,4,384]{2,1,0:T(4,128)S(1)}, f32[16,4,384]{2,1,0:T(4,128)S(1)}, u32[]{:S(2)}, u32[]{:S(2)}) collective-permute-start(f32[16,4,384]{2,1,0:T(4,128)S(1)} %get-tuple-element.17), channel_id=1, source_target_pairs={{0,1},{1,2},{2,3},{3,4},{4,5},{5,6},{6,7},{8,9},{9,10},{10,11},{11... | collective-permute-start | bytes 294920 | tf_op jit(solution)/shard_map/ppermute | solution.py:709
  7.8 7.8 %collective-permute-start.3 = (f32[16,4,384]{2,1,0:T(4,128)S(1)}, f32[16,4,384]{2,1,0:T(4,128)S(1)}, u32[]{:S(2)}, u32[]{:S(2)}) collective-permute-start(f32[16,4,384]{2,1,0:T(4,128)S(1)} %get-tuple-element.18), channel_id=1, source_target_pairs={{1,0},{2,1},{3,2},{4,3},{5,4},{6,5},{7,6},{9,8},{10,9},{11,10},{12... | collective-permute-start | bytes 294920 | tf_op jit(solution)/shard_map/ppermute | solution.py:709
  10.8 4.8 %copy-start.5 = (s32[1,1,16]{2,1,0:T(1,128)S(1)}, s32[1,1,16]{2,1,0:T(1,128)}, u32[]{:S(2)}) copy-start(s32[1,1,16]{2,1,0:T(1,128)} %start_ref.1) | copy-start | bytes 196
  38.7 13.6 %copy-start.6 = (f32[128,64,64]{0,2,1:T(8,128)S(1)}, f32[128,64,64]{0,2,1:T(8,128)}, u32[]{:S(2)}) copy-start(f32[128,64,64]{0,2,1:T(8,128)} %param.20) | copy-start | bytes 6291460
  39.6 32.1 %all-to-all-start.1 = ((f16[128,16,128]{2,1,0:T(8,128)(2,1)}), f16[128,16,128]{2,1,0:T(8,128)(2,1)}, u32[]{:S(2)}, u32[]{:S(2)}) async-start(f16[128,16,128]{2,1,0:T(8,128)(2,1)} %multiply_convert_fusion), calls=%async_computation.1 | async-start | bytes 1048576 | tf_op jit(solution)/shard_map/all_to_all | solution.py:747
  46.1 9.3 %collective-permute-start.4 = (f32[16,6,384]{2,1,0:T(8,128)S(1)}, f32[16,6,384]{2,1,0:T(8,128)S(1)}, u32[]{:S(2)}, u32[]{:S(2)}) collective-permute-start(f32[16,6,384]{2,1,0:T(8,128)S(1)} %get-tuple-element.24), channel_id=1, source_target_pairs={{0,1},{1,2},{2,3},{3,4},{4,5},{5,6},{6,7},{8,9},{9,10},{10,11},{11... | collective-permute-start | bytes 442376 | tf_op jit(solution)/shard_map/ppermute | solution.py:709
  49.2 11.2 %collective-permute-start.5 = (f32[16,6,384]{2,1,0:T(8,128)S(1)}, f32[16,6,384]{2,1,0:T(8,128)S(1)}, u32[]{:S(2)}, u32[]{:S(2)}) collective-permute-start(f32[16,6,384]{2,1,0:T(8,128)S(1)} %get-tuple-element.25), channel_id=1, source_target_pairs={{1,0},{2,1},{3,2},{4,3},{5,4},{6,5},{7,6},{9,8},{10,9},{11,10},{12... | collective-permute-start | bytes 442376 | tf_op jit(solution)/shard_map/ppermute | solution.py:709
where the time goes:
time: 74.3 us; the launch traced here: 73.8 us
  Pallas kernels  26.2 us (35%)
  starting transfers between devices  19.6 us (26%)
  blocking collectives  17 us (23%)
  waiting for transfers between devices  7.49 us (10%)
  other arithmetic  2.71 us (4%)
  between operations  0.88 us (1%)
    all_to_all x1, blocking collectives, per_device(): lax.all_to_all(outgoing, 'azimuth', split_axis=0, concat_axis=0, tiled=True)  17 us
    ppermute x6, starting transfers between devices, exchange(): return (lax.ppermute(last, axis, up), lax.ppermute(first, axis, down))  14.6 us
    pallas_call x1, Pallas kernels, fields_call(): pl.pallas_call(fields_kernel, name='fields', out_shape=jax.ShapeDtypeStru...  11.3 us
    ppermute x6, waiting for transfers between devices, exchange(): return (lax.ppermute(last, axis, up), lax.ppermute(first, axis, down))  7.48 us
    all_to_all x1, starting transfers between devices, per_device(): parts = lax.all_to_all(sends, BOTH, split_axis=0, concat_axis=0, tiled=True)  4.94 us
    pallas_call x1, Pallas kernels, panels_call(): pl.pallas_call(panels_kernel, name='panels', out_shape=(jax.ShapeDtypeStr...  4.7 us
    pallas_call x1, Pallas kernels, weights_call(): pl.pallas_call(weights_kernel, name='observers', out_shape=jax.ShapeDtype...  4.22 us
    pallas_call x2, Pallas kernels, pack_call(): pl.pallas_call(functools.partial(pack_kernel, rad=rad, with_az=with_az),...  3.17 us
  transfers between devices with their start and end apart: 7, of which 2 were waited for; matrix products, arithmetic and copies ran while one was open for 1% of the time, Pallas kernels for 24%

commit v1 on v0

--- a/solution.py
+++ b/solution.py
@@ -1,4 +1,3 @@
-import functools
 import math
 
 import jax
@@ -127,35 +126,36 @@
     return totals
 
 
-def pack_kernel(flow_ref, *refs, rad, with_az):
-    *outs, edge_ref, sems = refs
-    rad_first_ref, rad_last_ref = outs[-2:]
-    planes, rows = flow_ref.shape[1:3]
-    direct, edges = [], []
+def edge_copies(flow_ref, edge_ref, sems, rad):
+    copies = []
     for s, var in enumerate(rad):
-        for side, start in enumerate((0, rows - EDGE)):
-            edges.append(
-                pltpu.make_async_copy(
-                    flow_ref.at[var, :, pl.ds(start, EDGE)],
-                    edge_ref.at[side, s],
-                    sems.at[side, s],
-                )
-            )
-    if with_az:
-        for side, (ref, start) in enumerate(zip(outs, (0, planes - 2))):
-            direct.append(
-                pltpu.make_async_copy(
-                    flow_ref.at[:, pl.ds(start, 2)], ref, sems.at[side, len(rad)]
-                )
-            )
+        for side, start in enumerate((0, flow_ref.shape[2] - EDGE)):
+            src = flow_ref.at[var, :, pl.ds(start, EDGE)]
+            copies.append(pltpu.make_async_copy(src, edge_ref.at[side, s], sems.at[side, s]))
+    return copies
+
+
+def place_edges(edge_ref, first_ref, last_ref):
+    for a in range(edge_ref.shape[2]):
+        for s in range(edge_ref.shape[1]):
+            first_ref[a, 2 * s : 2 * s + 2, :] = edge_ref[0, s, a, 0:2, :]
+            last_ref[a, 2 * s : 2 * s + 2, :] = edge_ref[1, s, a, EDGE - 2 : EDGE, :]
+
+
+def pack_kernel(
+    flow_ref, az_first_ref, az_last_ref, rad_first_ref, rad_last_ref, edge_ref, sems, az_sems
+):
+    planes = flow_ref.shape[1]
+    edges = edge_copies(flow_ref, edge_ref, sems, FIRST_RAD)
+    direct = [
+        pltpu.make_async_copy(flow_ref.at[:, pl.ds(start, 2)], ref, az_sems.at[side])
+        for side, (ref, start) in enumerate(((az_first_ref, 0), (az_last_ref, planes - 2)))
+    ]
     for c in edges + direct:
         c.start()
     for c in edges:
         c.wait()
-    for a in range(planes):
-        for s in range(len(rad)):
-            rad_first_ref[a, 2 * s : 2 * s + 2, :] = edge_ref[0, s, a, 0:2, :]
-            rad_last_ref[a, 2 * s : 2 * s + 2, :] = edge_ref[1, s, a, EDGE - 2 : EDGE, :]
+    place_edges(edge_ref, rad_first_ref, rad_last_ref)
     for c in direct:
         c.wait()
 
@@ -198,13 +198,17 @@
     rows_ref,
     coef_ref,
     mask_ref,
+    first_ref,
+    last_ref,
     slots_ref,
     store_ref,
     wide_ref,
     block_ref,
+    edge_ref,
     rank_ref,
     own_ref,
     sems,
+    edge_sems,
 ):
     planes, tiles, band = store_ref.shape[1:4]
     sources = ((flow_ref, 4), (flow_ref, 1), (flow_ref, 2), (flow_ref, 3), (base_ref, 4))
@@ -218,7 +222,8 @@
     cycle, radius = lax.axis_index("azimuth"), lax.axis_index("radius")
     owners = pltpu.make_async_copy(owner_ref.at[cycle], own_ref, sems.at[len(sources), 0])
     owners.start()
-    for c in copies:
+    edges = edge_copies(flow_ref, edge_ref, edge_sems, LATER_RAD)
+    for c in copies + edges:
         c.start()
     mine = order_ref[cycle * lax.axis_size("radius") + radius]
     block = lax.broadcasted_iota(jnp.int32, mask_ref.shape, 1)
@@ -311,6 +316,9 @@
         return carry
 
     lax.fori_loop(0, count, local, 0)
+    for c in edges:
+        c.wait()
+    place_edges(edge_ref, first_ref, last_ref)
 
 
 def fresh_kernel(
@@ -505,22 +513,24 @@
     return pl.BlockSpec(shape, lambda *_: (0,) * len(shape))
 
 
-def pack_call(flow, rad, with_az):
+def pack_call(flow):
     nvar, planes, rows, length = flow.shape
     az_shape = jax.ShapeDtypeStruct((nvar, 2, rows, length), jnp.float32)
-    rad_shape = jax.ShapeDtypeStruct((planes, 2 * len(rad), length), jnp.float32)
-    shapes = (az_shape,) * (2 * with_az) + (rad_shape,) * 2
+    rad_shape = jax.ShapeDtypeStruct((planes, 2 * len(FIRST_RAD), length), jnp.float32)
+    shapes = (az_shape, az_shape, rad_shape, rad_shape)
     return pl.pallas_call(
-        functools.partial(pack_kernel, rad=rad, with_az=with_az),
+        pack_kernel,
+        name="pack",
         out_shape=shapes,
         in_specs=[ANY],
         out_specs=(IN_VMEM,) * len(shapes),
         scratch_shapes=[
-            pltpu.VMEM((2, len(rad), planes, EDGE, length), jnp.float32),
-            pltpu.SemaphoreType.DMA((2, len(rad) + 1)),
+            pltpu.VMEM((2, len(FIRST_RAD), planes, EDGE, length), jnp.float32),
+            pltpu.SemaphoreType.DMA((2, len(FIRST_RAD))),
+            pltpu.SemaphoreType.DMA((2,)),
         ],
         compiler_params=limits(8),
-        cost_estimate=cost(0, 20 * MIB),
+        cost_estimate=cost(0, 8 * nvar * 4 * rows * length),
     )(in_hbm(flow))
 
 
@@ -535,20 +545,23 @@
             jax.ShapeDtypeStruct((KMAX, 8, LANES), jnp.float32),
             jax.ShapeDtypeStruct((11, rows, LANES), jnp.float32),
             jax.ShapeDtypeStruct((1, order.shape[0]), jnp.float32),
+            *[jax.ShapeDtypeStruct((planes, 2 * len(LATER_RAD), length), jnp.float32)] * 2,
             jax.ShapeDtypeStruct((LANES,), jnp.int32),
         ),
         in_specs=[ANY, IN_SMEM, IN_SMEM, IN_VMEM, IN_SMEM, ANY, ANY, IN_VMEM],
-        out_specs=(IN_VMEM,) * 4 + (IN_SMEM,),
+        out_specs=(IN_VMEM,) * 6 + (IN_SMEM,),
         scratch_shapes=[
             pltpu.VMEM((5, planes, tiles, rows, LANES), jnp.float32),
             pltpu.VMEM((ROWS, KMAX, LANES), jnp.float32),
             pltpu.VMEM((ROWS, LANES), jnp.float32),
+            pltpu.VMEM((2, len(LATER_RAD), planes, EDGE, length), jnp.float32),
             pltpu.SMEM((owners,), jnp.int32),
             pltpu.SMEM(owner.shape[1:], jnp.int32),
             pltpu.SemaphoreType.DMA((6, tiles)),
+            pltpu.SemaphoreType.DMA((2, len(LATER_RAD))),
         ],
-        compiler_params=limits(8),
-        cost_estimate=cost(0, 5 * 4 * planes * rows * length),
+        compiler_params=limits(10),
+        cost_estimate=cost(0, 20 * MIB),
     )(in_hbm(owner), count, line, mean_flow, order, in_hbm(flow), in_hbm(base), history)
 
 
@@ -722,10 +735,10 @@
     retarded_time,
     observer_block,
 ):
-    az_first, az_last, *ends = pack_call(flow_state, FIRST_RAD, True)
+    az_first, az_last, *ends = pack_call(flow_state)
     az = exchange(az_first, az_last, "azimuth", True)
     rad0 = exchange(*ends, "radius", False)
-    history, local, coef, mask, slots = panels_call(
+    history, local, coef, mask, *later, slots = panels_call(
         panel_owner,
         panel_count.T,
         panel_line,
@@ -737,11 +750,8 @@
     )
     outgoing = fresh_call(slots, panel_line, panel_start, coef, local, az, rad0, history)
     stations = lax.all_to_all(outgoing, "azimuth", split_axis=0, concat_axis=0, tiled=True)
-    later, _ = lax.optimization_barrier((flow_state, outgoing))
-    packed = pack_call(later, LATER_RAD, False)
-    rad1 = exchange(*packed, "radius", False)
-    times, _ = lax.optimization_barrier((retarded_time, outgoing))
-    matrix = jnp.sum(times * mask[0][:, None, None], axis=0)
+    rad1 = exchange(*later, "radius", False)
+    matrix = jnp.sum(retarded_time * mask[0][:, None, None], axis=0)
     sends = weights_call(observer_block, stations, source_weight[0])
     sends = (WIRE_SCALE * sends).astype(jnp.float16)
     parts = lax.all_to_all(sends, BOTH, split_axis=0, concat_axis=0, tiled=True)

time: 74.3 us -> 73.1 us (0.984)
  Pallas kernels: 26.2 us -> 24.8 us
    reduce_sum x1, other arithmetic: 0.61 us -> 2.2 us  [per_device(): matrix = jnp.sum(retarded_time * mask[0][:, None, None], axis=0)]
    pallas_call x2 -> x1, Pallas kernels: 3.17 us -> 1.62 us  [pack_call(): pl.pallas_call(pack_kernel, name='pack', out_shape=shapes, in_specs=[ANY]...]
    reduce_sum x1, other arithmetic: 1.19 us -> 0.14 us  [per_device(): total = 1.0 / WIRE_SCALE * jnp.sum(parts.astype(jnp.float32), axis=0)]
  transfers between devices with their start and end apart: 7 -> 7, of which waited for: 2 -> 2; matrix products, arithmetic and copies ran while one was open for 1% -> 3% of each run, Pallas kernels for 24% -> 22%
where the time goes in v1:
time: 73.1 us; the launch traced here: 72.7 us
  Pallas kernels  24.8 us (34%)
  starting transfers between devices  19.1 us (26%)
  blocking collectives  17 us (23%)
  waiting for transfers between devices  7.65 us (10%)
  other arithmetic  3.26 us (4%)
  between operations  0.86 us (1%)
    all_to_all x1, blocking collectives, per_device(): lax.all_to_all(outgoing, 'azimuth', split_axis=0, concat_axis=0, tiled=True)  17 us
    ppermute x6, starting transfers between devices, exchange(): return (lax.ppermute(last, axis, up), lax.ppermute(first, axis, down))  14.6 us
    pallas_call x1, Pallas kernels, fields_call(): pl.pallas_call(fields_kernel, name='fields', out_shape=jax.ShapeDtypeStru...  11.3 us
    ppermute x6, waiting for transfers between devices, exchange(): return (lax.ppermute(last, axis, up), lax.ppermute(first, axis, down))  7.65 us
    pallas_call x1, Pallas kernels, panels_call(): pl.pallas_call(panels_kernel, name='panels', out_shape=(jax.ShapeDtypeStr...  4.89 us
    all_to_all x1, starting transfers between devices, per_device(): parts = lax.all_to_all(sends, BOTH, split_axis=0, concat_axis=0, tiled=True)  4.46 us
    pallas_call x1, Pallas kernels, weights_call(): pl.pallas_call(weights_kernel, name='observers', out_shape=jax.ShapeDtype...  4.22 us
    reduce_sum x1, other arithmetic, per_device(): matrix = jnp.sum(retarded_time * mask[0][:, None, None], axis=0)  2.2 us
  transfers between devices with their start and end apart: 7, of which 2 were waited for; matrix products, arithmetic and copies ran while one was open for 3% of the time, Pallas kernels for 22%

profile of v1, /device:TPU:3, one launch (start us, length us, event | category | flops | bytes accessed | tf_op | source)
XLA Modules:
  0.0 72.7 jit_solution(10929553547118213016)
XLA Ops:
  0.6 0.0 copy-start.3
  0.7 1.6 %pack.1 = (f32[5,2,32,384]{3,2,1,0:T(8,128)S(1)}, f32[5,2,32,384]{3,2,1,0:T(8,128)S(1)}, f32[16,4,384]{2,1,0:T(4,128)S(1)}, f32[16,4,384]{2,1,0:T(4,128)S(1)}) custom-call(f32[5,16,32,384]{3,2,1,0:T(8,128)} %flow_ref.5), custom_call_target="tpu_custom_call" | custom-call | bytes 1966080 | tf_op jit(solution)/shard_map/pack/pallas_call | solution.py:521
  2.3 2.3 %collective-permute-start = (f32[5,2,32,384]{3,2,1,0:T(8,128)S(1)}, f32[5,2,32,384]{3,2,1,0:T(8,128)S(1)}, u32[]{:S(2)}, u32[]{:S(2)}) collective-permute-start(f32[5,2,32,384]{3,2,1,0:T(8,128)S(1)} %get-tuple-element.13), channel_id=1, source_target_pairs={{0,8},{8,16},{16,24},{24,32},{32,40},{40,48},{48,56},{56,64},{64,7... | collective-permute-start | bytes 1474568 | tf_op jit(solution)/shard_map/ppermute | solution.py:722
  4.6 3.2 %collective-permute-start.2 = (f32[16,4,384]{2,1,0:T(4,128)S(1)}, f32[16,4,384]{2,1,0:T(4,128)S(1)}, u32[]{:S(2)}, u32[]{:S(2)}) collective-permute-start(f32[16,4,384]{2,1,0:T(4,128)S(1)} %get-tuple-element.15), channel_id=1, source_target_pairs={{0,1},{1,2},{2,3},{3,4},{4,5},{5,6},{6,7},{8,9},{9,10},{10,11},{11... | collective-permute-start | bytes 294920 | tf_op jit(solution)/shard_map/ppermute | solution.py:722
  7.8 3.0 %collective-permute-start.3 = (f32[16,4,384]{2,1,0:T(4,128)S(1)}, f32[16,4,384]{2,1,0:T(4,128)S(1)}, u32[]{:S(2)}, u32[]{:S(2)}) collective-permute-start(f32[16,4,384]{2,1,0:T(4,128)S(1)} %get-tuple-element.16), channel_id=1, source_target_pairs={{1,0},{2,1},{3,2},{4,3},{5,4},{6,5},{7,6},{9,8},{10,9},{11,10},{12... | collective-permute-start | bytes 294920 | tf_op jit(solution)/shard_map/ppermute | solution.py:722
  10.8 0.0 copy-start.5
  10.8 4.9 %panels.1 = (bf16[16,32,128]{2,1,0:T(8,128)(2,1)S(1)}, f32[16,8,128]{2,1,0:T(8,128)S(1)}, f32[11,32,128]{2,1,0:T(8,128)S(1)}, f32[1,128]{1,0:T(1,128)S(1)}, f32[...) custom-call(s32[16,8,16]{2,1,0:T(8,128)} %owner_ref.1, s32[8,16]{1,0:T(8,128)S(1)} %bitcast.6, ...), custom_call_target="tpu_custom_call" | custom-call | bytes 20971520 | tf_op jit(solution)/shard_map/panels/pallas_call | solution.py:540
  15.7 0.0 collective-permute-done.2.lo0_ref.lo_ref
  15.7 0.0 collective-permute-done.3.hi0_ref.hi_ref
  15.8 0.0 collective-permute-done.1.after_ref
  15.8 1.8 %fresh.1 = bf16[16,32,128]{2,1,0:T(8,128)(2,1)S(1)} custom-call(s32[128]{0:T(128)S(1)} %get-tuple-element.20.slots_ref, s32[1,1,16]{2,1,0:T(1,128)S(1)} %copy-done.2, s32[1,1,16]{2,1,0:T(1,128)S(1)} %copy-done.5, f32[11,32,128]{2,1,0:T(8,128)S(1)} %get-tuple-element.19.coef_ref, f32[16,8,128]{2,1,0:T(8,128)S(1)} %get-tuple-element.21.rows_ref, ...), custom_call_target="tpu_custom_call" | custom-call | bytes 786432 | tf_op jit(solution)/shard_map/fresh/pallas_call | solution.py:571
  17.6 17.0 %all_to_all.10.stations_ref = bf16[16,32,128]{2,1,0:T(8,128)(2,1)S(1)} all-to-all(bf16[16,32,128]{2,1,0:T(8,128)(2,1)S(1)} %fresh.1), channel_id=1, replica_groups=mesh['azimuth'=16,'radius'=8] {'azimuth'}, dimensions={0} | all-to-all | bytes 262144 | tf_op jit(solution)/shard_map/all_to_all | solution.py:752
  34.6 4.2 %observers.1 = f32[128,16,128]{2,1,0:T(8,128)S(1)} custom-call(bf16[16,32,128]{2,1,0:T(8,128)(2,1)S(1)} %all_to_all.10.stations_ref, s32[128]{0:T(128)} %order_ref.3, bf16[1024,4096]{1,0:T(8,128)(2,1)} %bitcast.8), custom_call_target="tpu_custom_call" | custom-call | flops 536870912 | bytes 8388608 | tf_op jit(solution)/shard_map/observers/pallas_call | solution.py:668
  38.8 0.9 %multiply_convert_fusion = f16[128,16,128]{2,1,0:T(8,128)(2,1)} fusion(f32[128,16,128]{2,1,0:T(8,128)S(1)} %observers.1), kind=kLoop, calls=%fused_computation.2 | loop fusion | flops 524288 | bytes 1572864 | tf_op jit(solution)/shard_map/convert_element_type | solution.py:756
  39.7 4.5 %all-to-all-start.1 = ((f16[128,16,128]{2,1,0:T(8,128)(2,1)}), f16[128,16,128]{2,1,0:T(8,128)(2,1)S(1)}, u32[]{:S(2)}, u32[]{:S(2)}) async-start(f16[128,16,128]{2,1,0:T(8,128)(2,1)} %multiply_convert_fusion), calls=%async_computation.1 | async-start | bytes 1048576 | tf_op jit(solution)/shard_map/all_to_all | solution.py:757
  44.2 3.1 %collective-permute-start.4 = (f32[16,6,384]{2,1,0:T(8,128)S(1)}, f32[16,6,384]{2,1,0:T(8,128)S(1)}, u32[]{:S(2)}, u32[]{:S(2)}) collective-permute-start(f32[16,6,384]{2,1,0:T(8,128)S(1)} %get-tuple-element.17), channel_id=1, source_target_pairs={{0,1},{1,2},{2,3},{3,4},{4,5},{5,6},{6,7},{8,9},{9,10},{10,11},{11... | collective-permute-start | bytes 442376 | tf_op jit(solution)/shard_map/ppermute | solution.py:722
  47.3 3.1 %collective-permute-start.5 = (f32[16,6,384]{2,1,0:T(8,128)S(1)}, f32[16,6,384]{2,1,0:T(8,128)S(1)}, u32[]{:S(2)}, u32[]{:S(2)}) collective-permute-start(f32[16,6,384]{2,1,0:T(8,128)S(1)} %get-tuple-element.18), channel_id=1, source_target_pairs={{1,0},{2,1},{3,2},{4,3},{5,4},{6,5},{7,6},{9,8},{10,9},{11,10},{12... | collective-permute-start | bytes 442376 | tf_op jit(solution)/shard_map/ppermute | solution.py:722
  50.4 2.2 %multiply_reduce_fusion.matrix_ref = f32[64,64]{1,0:T(8,128)S(1)} fusion(f32[128,64,64]{0,2,1:T(8,128)} %param.20, f32[128]{0:T(128)S(1)} %bitcast.7), kind=kLoop, calls=%fused_computation | loop fusion | flops 1044480 | bytes 2114048 | tf_op jit(solution)/shard_map/reduce_sum | solution.py:754
  52.6 5.2 %collective-permute-done.4.lo1_ref = f32[16,6,384]{2,1,0:T(8,128)S(1)} collective-permute-done((f32[16,6,384]{2,1,0:T(8,128)S(1)}, f32[16,6,384]{2,1,0:T(8,128)S(1)}, u32[]{:S(2)}, u32[]{:S(2)}) %collective-permute-start.4) | collective-permute-done | bytes 147488 | tf_op jit(solution)/shard_map/ppermute | solution.py:722
  57.9 2.4 %collective-permute-done.5.hi1_ref = f32[16,6,384]{2,1,0:T(8,128)S(1)} collective-permute-done((f32[16,6,384]{2,1,0:T(8,128)S(1)}, f32[16,6,384]{2,1,0:T(8,128)S(1)}, u32[]{:S(2)}, u32[]{:S(2)}) %collective-permute-start.5) | collective-permute-done | bytes 147488 | tf_op jit(solution)/shard_map/ppermute | solution.py:722
  60.3 11.3 %fields.1 = f32[5,16,32,384]{3,2,1,0:T(8,128)} custom-call(f32[5,16,32,384]{3,2,1,0:T(8,128)} %flow_ref.5, f32[5,2,32,384]{3,2,1,0:T(8,128)S(1)} %collective-permute-done.before_ref, f32[5,2,32,384]{3,2,1,0:T(8,128)S(1)} %collective-permute-done.1.after_ref, f32[5,16,32,384]{3,2,1,0:T(8,128)} %base_ref.3, ...), custom_call_target="tpu_custom_call" | custom-call | flops 49152000 | bytes 11796480 | tf_op jit(solution)/shard_map/fields/pallas_call | solution.py:592
  71.6 0.0 all-to-all-done.1
  71.6 0.1 convert_reduce_fusion
  71.8 0.9 %retard.1 = f32[16,128]{1,0:T(8,128)} custom-call(f32[16,128]{1,0:T(8,128)S(1)} %broadcast_multiply_fusion.total_ref, f32[64,64]{1,0:T(8,128)S(1)} %multiply_reduce_fusion.matrix_ref), custom_call_target="tpu_custom_call" | custom-call | flops 1048576 | bytes 16384 | tf_op jit(solution)/shard_map/retard/pallas_call | solution.py:706
  (13 shorter events, 0.0 us)
Async XLA Ops:
  0.6 10.1 %copy-start.3 = (s32[128]{0:T(128)S(1)}, s32[128]{0:T(128)}, u32[]{:S(2)}) copy-start(s32[128]{0:T(128)} %order_ref.3) | copy-start | bytes 1540
  0.6 10.1 %copy-start.2 = (s32[1,1,16]{2,1,0:T(1,128)S(1)}, s32[1,1,16]{2,1,0:T(1,128)}, u32[]{:S(2)}) copy-start(s32[1,1,16]{2,1,0:T(1,128)} %line_ref.3) | copy-start | bytes 196
  0.7 10.1 %copy-start.1 = (s32[16,8]{0,1:T(8,128)S(1)}, s32[16,8]{0,1:T(8,128)}, u32[]{:S(2)}) copy-start(s32[16,8]{0,1:T(8,128)} %param.17) | copy-start | bytes 1540
  0.7 10.1 %copy-start = (bf16[1,1,16,2016]{3,2,1,0:T(8,128)(2,1)S(1)}, bf16[1,1,16,2016]{3,2,1,0:T(8,128)(2,1)}, u32[]{:S(2)}) copy-start(bf16[1,1,16,2016]{3,2,1,0:T(8,128)(2,1)} %param.14) | copy-start | bytes 193540
  0.7 10.1 %copy-start.4 = (f32[2,32]{1,0:T(2,128)S(1)}, f32[2,32]{1,0:T(2,128)}, u32[]{:S(2)}) copy-start(f32[2,32]{1,0:T(2,128)} %mean_ref.1) | copy-start | bytes 772
  2.3 13.4 %collective-permute-start = (f32[5,2,32,384]{3,2,1,0:T(8,128)S(1)}, f32[5,2,32,384]{3,2,1,0:T(8,128)S(1)}, u32[]{:S(2)}, u32[]{:S(2)}) collective-permute-start(f32[5,2,32,384]{3,2,1,0:T(8,128)S(1)} %get-tuple-element.13), channel_id=1, source_target_pairs={{0,8},{8,16},{16,24},{24,32},{32,40},{40,48},{48,56},{56,64},{64,7... | collective-permute-start | bytes 1474568 | tf_op jit(solution)/shard_map/ppermute | solution.py:722
  4.6 11.2 %collective-permute-start.1 = (f32[5,2,32,384]{3,2,1,0:T(8,128)S(1)}, f32[5,2,32,384]{3,2,1,0:T(8,128)S(1)}, u32[]{:S(2)}, u32[]{:S(2)}) collective-permute-start(f32[5,2,32,384]{3,2,1,0:T(8,128)S(1)} %get-tuple-element.14), channel_id=1, source_target_pairs={{8,0},{16,8},{24,16},{32,24},{40,32},{48,40},{56,48},{64,56},{72,6... | collective-permute-start | bytes 1474568 | tf_op jit(solution)/shard_map/ppermute | solution.py:722
  4.6 11.2 %collective-permute-start.2 = (f32[16,4,384]{2,1,0:T(4,128)S(1)}, f32[16,4,384]{2,1,0:T(4,128)S(1)}, u32[]{:S(2)}, u32[]{:S(2)}) collective-permute-start(f32[16,4,384]{2,1,0:T(4,128)S(1)} %get-tuple-element.15), channel_id=1, source_target_pairs={{0,1},{1,2},{2,3},{3,4},{4,5},{5,6},{6,7},{8,9},{9,10},{10,11},{11... | collective-permute-start | bytes 294920 | tf_op jit(solution)/shard_map/ppermute | solution.py:722
  7.8 8.0 %collective-permute-start.3 = (f32[16,4,384]{2,1,0:T(4,128)S(1)}, f32[16,4,384]{2,1,0:T(4,128)S(1)}, u32[]{:S(2)}, u32[]{:S(2)}) collective-permute-start(f32[16,4,384]{2,1,0:T(4,128)S(1)} %get-tuple-element.16), channel_id=1, source_target_pairs={{1,0},{2,1},{3,2},{4,3},{5,4},{6,5},{7,6},{9,8},{10,9},{11,10},{12... | collective-permute-start | bytes 294920 | tf_op jit(solution)/shard_map/ppermute | solution.py:722
  10.8 5.0 %copy-start.5 = (s32[1,1,16]{2,1,0:T(1,128)S(1)}, s32[1,1,16]{2,1,0:T(1,128)}, u32[]{:S(2)}) copy-start(s32[1,1,16]{2,1,0:T(1,128)} %start_ref.1) | copy-start | bytes 196
  39.7 31.9 %all-to-all-start.1 = ((f16[128,16,128]{2,1,0:T(8,128)(2,1)}), f16[128,16,128]{2,1,0:T(8,128)(2,1)S(1)}, u32[]{:S(2)}, u32[]{:S(2)}) async-start(f16[128,16,128]{2,1,0:T(8,128)(2,1)} %multiply_convert_fusion), calls=%async_computation.1 | async-start | bytes 1048576 | tf_op jit(solution)/shard_map/all_to_all | solution.py:757
  44.2 13.6 %collective-permute-start.4 = (f32[16,6,384]{2,1,0:T(8,128)S(1)}, f32[16,6,384]{2,1,0:T(8,128)S(1)}, u32[]{:S(2)}, u32[]{:S(2)}) collective-permute-start(f32[16,6,384]{2,1,0:T(8,128)S(1)} %get-tuple-element.17), channel_id=1, source_target_pairs={{0,1},{1,2},{2,3},{3,4},{4,5},{5,6},{6,7},{8,9},{9,10},{10,11},{11... | collective-permute-start | bytes 442376 | tf_op jit(solution)/shard_map/ppermute | solution.py:722
  47.3 12.9 %collective-permute-start.5 = (f32[16,6,384]{2,1,0:T(8,128)S(1)}, f32[16,6,384]{2,1,0:T(8,128)S(1)}, u32[]{:S(2)}, u32[]{:S(2)}) collective-permute-start(f32[16,6,384]{2,1,0:T(8,128)S(1)} %get-tuple-element.18), channel_id=1, source_target_pairs={{1,0},{2,1},{3,2},{4,3},{5,4},{6,5},{7,6},{9,8},{10,9},{11,10},{12... | collective-permute-start | bytes 442376 | tf_op jit(solution)/shard_map/ppermute | solution.py:722
